TPU v7x, 128 devices: a whole 4x4x4 slice. The times are simulated.
128 devices in a mesh: section: 2 (over x_hi), dp: 8 (over z, core), mp: 8 (over x_lo, y).
Axes of the slice: x: 4 (x_hi: 2, x_lo: 2; x = x_hi * 2 + x_lo), y: 4, z: 4, core: 2. Of those that a mesh axis runs over, the one named last changes fastest.
Arguments:
- inputs: bfloat16 [2, 16, 128, 4096], P('section', 'dp'), may hold values from -6 to 6
- norm_gains: bfloat16 [2, 4096], P('section'), may hold values from 0.5 to 1.5
- weights: bfloat16 [2, 4096, 4, 4096], P('section', 'dp', None, 'mp'), may hold values from -0.09375 to 0.09375
- cotangent: bfloat16 [16, 128, 4096], P('dp'), may hold values from -6 to 6
- lengths: int32 [2, 16], P(None, 'dp'), may hold values from 32 to 128, as said below
- dp_noise: float32 [2, 4096, 4, 4096], P('section', 'dp', None, 'mp'), may hold values from -6 to 6
Outputs:
- noisy_grad: float32 [2, 4096, 4, 4096], P('section', 'dp', None, 'mp')
- clip_scale: float32 [16], P('dp')
Inputs may be any that keep to these rules, and one draw needn't show every extreme that they name: `lengths`: the first example of each row has length 128.
All inputs are finite; a program needn't handle non-finite values.
Results may differ from a plain program's by a relative error of at most 0.024.
Values may be sent and summed in bfloat16 or wider, within the bound.
A program may use at most 256 MiB of HBM per device.

v0:
```python
import jax
import jax.numpy as jnp
from jax import lax
from jax.sharding import PartitionSpec as P

D = 4096
HEADS = 64
HEAD = 64


def from_partner(x, axis, distance):
    return lax.ppermute(x, axis, [(i, i ^ 1 << distance) for i in range(lax.axis_size(axis))])


def rms_norm(values_in, gain_row):
    value32 = values_in.astype(jnp.float32)
    inverse = lax.rsqrt(jnp.mean(value32 * value32, axis=-1, keepdims=True) + 1e-06)
    return (value32 * inverse * gain_row.astype(jnp.float32)).astype(jnp.bfloat16)


def project(left, right):
    return jnp.dot(left, right, preferred_element_type=jnp.float32).astype(jnp.bfloat16)


def attend(queries, key_proj, value_proj, key_mask):
    seq_len = queries.shape[0]
    query_heads = queries.reshape(seq_len, -1, HEAD)
    key_heads = key_proj.reshape(seq_len, -1, HEAD)
    value_heads = value_proj.reshape(seq_len, -1, HEAD)
    scores = jnp.einsum(
        "shd,thd->hst", query_heads, key_heads, preferred_element_type=jnp.float32
    ) * HEAD ** (-0.5)
    scores = jnp.where(key_mask[None, None, :], scores, -jnp.inf)
    attn_probs = jax.nn.softmax(scores, axis=-1)
    probs_low = attn_probs.astype(jnp.bfloat16)
    context = jnp.einsum("hst,thd->shd", probs_low, value_heads, preferred_element_type=jnp.float32)
    return (attn_probs, context.reshape(seq_len, -1).astype(jnp.bfloat16))


def attend_back(queries, key_proj, value_proj, attn_probs, grad_ctx):
    seq_len = queries.shape[0]
    query_heads = queries.reshape(seq_len, -1, HEAD)
    key_heads = key_proj.reshape(seq_len, -1, HEAD)
    value_heads = value_proj.reshape(seq_len, -1, HEAD)
    grad_heads = grad_ctx.reshape(seq_len, -1, HEAD)
    grad_probs = jnp.einsum(
        "shd,thd->hst", grad_heads, value_heads, preferred_element_type=jnp.float32
    )
    inner_sum = jnp.sum(grad_probs * attn_probs, axis=-1, keepdims=True)
    grad_scores = (attn_probs * (grad_probs - inner_sum) * HEAD ** (-0.5)).astype(jnp.bfloat16)
    probs_low = attn_probs.astype(jnp.bfloat16)
    grad_query = jnp.einsum(
        "hst,thd->shd", grad_scores, key_heads, preferred_element_type=jnp.float32
    )
    grad_key = jnp.einsum(
        "hst,shd->thd", grad_scores, query_heads, preferred_element_type=jnp.float32
    )
    grad_value = jnp.einsum(
        "hst,shd->thd", probs_low, grad_heads, preferred_element_type=jnp.float32
    )
    return (
        grad_query.reshape(seq_len, -1).astype(jnp.bfloat16),
        grad_key.reshape(seq_len, -1).astype(jnp.bfloat16),
        grad_value.reshape(seq_len, -1).astype(jnp.bfloat16),
    )


def gram(matrix):
    return jnp.dot(matrix, matrix.T, preferred_element_type=jnp.float32)


def ghost(normed, kv_rows, grad_query, grad_key, grad_value, grad_out, context):
    first = jnp.sum(gram(normed) * gram(grad_query))
    second = jnp.sum(gram(kv_rows) * (gram(grad_key) + gram(grad_value)))
    third = jnp.sum(gram(grad_out) * gram(context))
    return first + second + third


def get_row(buffer, index):
    return lax.dynamic_index_in_dim(buffer, index, 0, keepdims=False)


def put_row(buffer, value, index, valid):
    current = get_row(buffer, index)
    return lax.dynamic_update_index_in_dim(buffer, jnp.where(valid, value, current), index, 0)


def per_device(inputs, norm_gains, weights, cotangent, lengths, dp_noise):
    section_index = lax.axis_index("section")
    is_dec = section_index == 1
    micro_count = inputs.shape[1]
    seq_len = inputs.shape[2]
    width = inputs.shape[3]
    gathered = lax.all_gather(weights, "dp", axis=1, tiled=True)[0]
    inner_dev = gathered.shape[2]
    own_inputs = inputs[0]
    gain_row = norm_gains[0]
    positions = jnp.arange(seq_len)
    wide_zero = jnp.zeros((micro_count, seq_len, width), jnp.bfloat16)
    thin_zero = jnp.zeros((micro_count, seq_len, inner_dev), jnp.bfloat16)
    normed_buf, kv_buf, gout_buf = (wide_zero, wide_zero, wide_zero)
    query_buf, key_buf, value_buf, context_buf = (thin_zero, thin_zero, thin_zero, thin_zero)
    gq_buf, gk_buf, gv_buf = (thin_zero, thin_zero, thin_zero)
    probs_buf = jnp.zeros((micro_count, inner_dev // HEAD, seq_len, seq_len), jnp.float32)
    norm_parts = jnp.zeros((micro_count,), jnp.float32)
    incoming = jnp.zeros((seq_len, width), jnp.bfloat16)
    for step_num in range(micro_count + 2):
        fwd_mb = step_num - section_index
        fwd_ok = (fwd_mb >= 0) & (fwd_mb < micro_count)
        fwd_idx = jnp.clip(fwd_mb, 0, micro_count - 1)
        rows_now = get_row(own_inputs, fwd_idx)
        normed = rms_norm(rows_now, gain_row)
        kv_rows = jnp.where(is_dec, incoming, normed)
        queries = project(normed, gathered[:, 0])
        key_proj = project(kv_rows, gathered[:, 1])
        value_proj = project(kv_rows, gathered[:, 2])
        key_mask = positions < get_row(lengths[0], fwd_idx)
        attn_probs, context_new = attend(queries, key_proj, value_proj, key_mask)
        normed_buf = put_row(normed_buf, normed, fwd_idx, fwd_ok)
        kv_buf = put_row(kv_buf, kv_rows, fwd_idx, fwd_ok)
        query_buf = put_row(query_buf, queries, fwd_idx, fwd_ok)
        key_buf = put_row(key_buf, key_proj, fwd_idx, fwd_ok)
        value_buf = put_row(value_buf, value_proj, fwd_idx, fwd_ok)
        probs_buf = put_row(probs_buf, attn_probs, fwd_idx, fwd_ok)
        context_buf = put_row(context_buf, context_new, fwd_idx, fwd_ok)
        bwd_mb = step_num - 2 + section_index
        bwd_ok = (bwd_mb >= 0) & (bwd_mb < micro_count)
        bwd_idx = jnp.clip(bwd_mb, 0, micro_count - 1)
        dec_mask = (positions < get_row(lengths[1], bwd_idx)).astype(jnp.bfloat16)
        cot_rows = get_row(cotangent, bwd_idx) * dec_mask[:, None]
        grad_out = jnp.where(is_dec, cot_rows, incoming)
        grad_ctx = project(grad_out, gathered[:, 3])
        back_query = get_row(query_buf, bwd_idx)
        back_key = get_row(key_buf, bwd_idx)
        back_value = get_row(value_buf, bwd_idx)
        back_context = get_row(context_buf, bwd_idx)
        grad_query, grad_key, grad_value = attend_back(
            back_query, back_key, back_value, get_row(probs_buf, bwd_idx), grad_ctx
        )
        sq_part = ghost(
            get_row(normed_buf, bwd_idx),
            get_row(kv_buf, bwd_idx),
            grad_query,
            grad_key,
            grad_value,
            grad_out,
            back_context,
        )
        gout_buf = put_row(gout_buf, grad_out, bwd_idx, bwd_ok)
        gq_buf = put_row(gq_buf, grad_query, bwd_idx, bwd_ok)
        gk_buf = put_row(gk_buf, grad_key, bwd_idx, bwd_ok)
        gv_buf = put_row(gv_buf, grad_value, bwd_idx, bwd_ok)
        slot_hit = bwd_ok & (jnp.arange(micro_count) == bwd_idx)
        norm_parts = jnp.where(slot_hit, sq_part, norm_parts)
        if step_num < micro_count + 1:
            relay_term = lax.cond(
                is_dec,
                lambda: jnp.einsum(
                    "sj,dj->sd", grad_key, gathered[:, 1], preferred_element_type=jnp.float32
                )
                + jnp.einsum(
                    "sj,dj->sd", grad_value, gathered[:, 2], preferred_element_type=jnp.float32
                ),
                lambda: jnp.einsum(
                    "sj,dj->sd", context_new, gathered[:, 3], preferred_element_type=jnp.float32
                ),
            )
            residual = jnp.where(is_dec, 0.0, rows_now.astype(jnp.float32))
            summed_rows = lax.psum(relay_term.astype(jnp.bfloat16), "mp").astype(jnp.float32)
            payload = (summed_rows + residual).astype(jnp.bfloat16)
            incoming = from_partner(payload, "section", 0)
    sq_norm = lax.psum(norm_parts, ("section", "mp"))
    bound = jnp.sqrt(jnp.float32(8.0 * D * HEADS * HEAD))
    clip_scale = bound / (jnp.sqrt(sq_norm) + 0.01 * bound)
    totals = jnp.zeros((weights.shape[1] * lax.axis_size("dp"), 4, inner_dev), jnp.float32)
    for micro_num in range(micro_count):
        normed_cols = normed_buf[micro_num]
        kv_cols = kv_buf[micro_num]
        gout_cols = gout_buf[micro_num]
        stacked = jnp.stack(
            [
                jnp.einsum(
                    "sd,sj->dj", normed_cols, gq_buf[micro_num], preferred_element_type=jnp.float32
                ),
                jnp.einsum(
                    "sd,sj->dj", kv_cols, gk_buf[micro_num], preferred_element_type=jnp.float32
                ),
                jnp.einsum(
                    "sd,sj->dj", kv_cols, gv_buf[micro_num], preferred_element_type=jnp.float32
                ),
                jnp.einsum(
                    "sd,sj->dj",
                    gout_cols,
                    context_buf[micro_num],
                    preferred_element_type=jnp.float32,
                ),
            ],
            axis=1,
        )
        totals = totals + clip_scale[micro_num] * stacked
    summed = lax.psum_scatter(
        totals.astype(jnp.bfloat16), "dp", scatter_dimension=0, tiled=True
    ).astype(jnp.float32)
    examples_total = micro_count * lax.axis_size("dp")
    noisy_grad = (summed + dp_noise[0]) / examples_total
    return (noisy_grad[None], clip_scale)


def solution(mesh):
    placed = (
        P("section", "dp", None, None),
        P("section", None),
        P("section", "dp", None, "mp"),
        P("dp", None, None),
        P(None, "dp"),
        P("section", "dp", None, "mp"),
    )
    return jax.shard_map(
        per_device,
        mesh=mesh,
        in_specs=placed,
        out_specs=(P("section", "dp", None, "mp"), P("dp")),
        check_vma=False,
    )
```

profile of v0, /device:TPU:1, one launch (start us, length us, event | category | flops | bytes accessed | tf_op | source)
XLA Modules:
  0.0 845.7 jit_solution(15828079697014097432)
XLA Ops:
  7.2 3.3 copy.83
  24.2 2.9 fusion.165
  38.8 60.7 %all-gather.2.cloned.1.call-done = bf16[1,4096,4,512]{3,1,2,0:T(8,128)(2,1)} async-done(((bf16[1,512,4,512]{3,1,2,0:T(8,128)(2,1)}), bf16[1,4096,4,512]{3,1,2,0:T(8,128)(2,1)}) %all-gather.2.cloned.1.call-update) | async-done | bytes 16777232 | tf_op jit(solution)/shard_map/all_gather | solution.py:94
  99.5 3.3 fusion.125
  103.5 3.6 bitcast_dynamic-update-slice_fusion.20
  107.2 3.0 bitcast_dynamic-update-slice_fusion.21
  112.5 3.0 bitcast_dynamic-update-slice_fusion.19
  130.8 4.8 conditional.3
  130.8 4.8 fusion
  148.2 63.0 %all-reduce.4.cloned.1.call-done = bf16[128,4096]{1,0:T(8,128)(2,1)} async-done(((bf16[128,4096]{1,0:T(8,128)(2,1)}), bf16[128,4096]{1,0:T(8,128)(2,1)}) %all-reduce.4.cloned.1.call-update) | async-done | bytes 1048592 | tf_op jit(solution)/shard_map/psum | solution.py:169
  211.2 3.8 fusion.60
  215.5 3.6 bitcast_dynamic-update-slice_fusion.17
  221.2 3.0 fusion.132
  227.3 3.6 fusion.131
  245.4 6.0 bitcast_dynamic-update-slice_fusion.5
  252.5 3.7 fusion.138
  262.4 3.8 bitcast_dynamic-update-slice_fusion.16
  267.0 3.2 fusion.126
  299.0 4.9 conditional.4
  299.0 4.8 fusion.8
  315.2 70.6 %all-reduce.6.cloned.1.call-done = bf16[128,4096]{1,0:T(8,128)(2,1)} async-done(((bf16[128,4096]{1,0:T(8,128)(2,1)}), bf16[128,4096]{1,0:T(8,128)(2,1)}) %all-reduce.6.cloned.1.call-update) | async-done | bytes 1048592 | tf_op jit(solution)/shard_map/psum | solution.py:169
  395.2 12.4 %collective-permute-done.1 = bf16[128,4096]{1,0:T(8,128)(2,1)S(1)} collective-permute-done((bf16[128,4096]{1,0:T(8,128)(2,1)S(1)}, bf16[128,4096]{1,0:T(8,128)(2,1)S(1)}, u32[]{:S(2)}, u32[]{:S(2)}) %collective-permute-start.1) | collective-permute-done | bytes 1048608 | tf_op jit(solution)/shard_map/ppermute | solution.py:12
  407.6 4.8 bitcast_dynamic-update-slice_fusion.4
  413.4 3.7 fusion.139
  423.4 3.9 bitcast_dynamic-update-slice_fusion.13
  438.9 3.2 fusion.127
  460.9 4.8 conditional.5
  460.9 4.8 fusion.16
  476.4 72.0 %all-reduce.8.cloned.1.call-done = bf16[128,4096]{1,0:T(8,128)(2,1)} async-done(((bf16[128,4096]{1,0:T(8,128)(2,1)}), bf16[128,4096]{1,0:T(8,128)(2,1)}) %all-reduce.8.cloned.1.call-update) | async-done | bytes 1048592 | tf_op jit(solution)/shard_map/psum | solution.py:169
  550.0 2.9 collective-permute-start.2
  558.3 12.4 %collective-permute-done.2 = bf16[128,4096]{1,0:T(8,128)(2,1)S(1)} collective-permute-done((bf16[128,4096]{1,0:T(8,128)(2,1)S(1)}, bf16[128,4096]{1,0:T(8,128)(2,1)S(1)}, u32[]{:S(2)}, u32[]{:S(2)}) %collective-permute-start.2) | collective-permute-done | bytes 1048608 | tf_op jit(solution)/shard_map/ppermute | solution.py:12
  570.7 4.8 bitcast_dynamic-update-slice_fusion.3
  576.5 3.0 fusion.140
  581.9 4.0 bitcast_dynamic-update-slice_fusion.11
  585.9 3.6 fusion.128
  604.4 5.7 convolution_bitcast_fusion.1
  610.1 5.7 convolution_bitcast_fusion.5
  615.8 5.7 convolution_bitcast_fusion.2
  621.5 5.7 convolution_bitcast_fusion.6
  629.2 5.9 convolution_bitcast_fusion
  635.1 5.7 convolution_bitcast_fusion.4
  654.0 5.7 convolution_bitcast_fusion.3
  662.1 5.8 convolution_bitcast_fusion.7
  667.9 31.8 %psum.31 = f32[2]{0:T(128)S(1)} all-reduce(f32[2]{0:T(128)S(1)} %and_select_fusion.3), channel_id=1, replica_groups=mesh['section'=2,'dp'=8,'mp'=8] {'section','mp'}, use_global_device_ids=true, to_apply=%region_37.38 | all-reduce | flops 2 | bytes 16 | tf_op jit(solution)/shard_map/psum | solution.py:172
  700.3 28.8 %fusion.33 = bf16[4096,4,512]{2,0,1:T(8,128)(2,1)} fusion(f32[4096,1,512]{2,0,1:T(8,128)} %convolution_bitcast_fusion.4, f32[4096,1,512]{2,0,1:T(8,128)} %convolution_bitcast_fusion.5, f32[4096,1,512]{2,0,1:T(8,128)} %convolution_bitcast_fusion.6, f32[4096,1,512]{2,0,1:T(8,128)} %convolution_bitcast_fusion.7, f32[4096,1,512]{2,0,1:T(8,128)} %convolution_bitcast_fusion, ...), kind=kLoop, calls=%fused_computation.37 | loop fusion | flops 83886080 | bytes 83886088 | tf_op jit(solution)/shard_map/convert_element_type | solution.py:202
  729.1 100.7 %reduce-scatter.2.cloned.1.call-done = bf16[512,4,512]{2,0,1:T(8,128)(2,1)} async-done(((bf16[4096,4,512]{2,0,1:T(8,128)(2,1)}), bf16[512,4,512]{2,0,1:T(8,128)(2,1)}) %reduce-scatter.2.cloned.1.call-update) | async-done | bytes 2097168 | tf_op jit(solution)/shard_map/reduce_scatter | solution.py:201
  829.9 4.4 fusion.35
  834.3 4.7 copy.145
  (290 shorter events, 218.2 us)
Async XLA Ops:
  7.2 92.3 %all-gather.2.cloned.1.call-start = ((), (), s32[]{:S(2)}) async-start(), calls=%async_computation.1 | async-start | bytes 18874368 | tf_op jit(solution)/shard_map/all_gather | solution.py:94
  10.6 200.7 %all-reduce.4.cloned.1.call-start = ((), (), s32[]{:S(2)}) async-start(), calls=%async_computation.2 | async-start | bytes 2097152 | tf_op jit(solution)/shard_map/psum | solution.py:169
  21.3 86.0 %copy-start.38 = (f32[128]{0:T(128)}, f32[128]{0:T(128)S(1)}, u32[]{:S(2)}) copy-start(f32[128]{0:T(128)S(1)} %add_rsqrt_fusion.3) | copy-start | bytes 1540
  22.9 4.3 copy-start.3
  110.2 6.1 copy-start.8
  115.5 5.8 copy-start.6
  135.6 250.2 %all-reduce.6.cloned.1.call-start = ((), (), s32[]{:S(2)}) async-start(), calls=%async_computation.3 | async-start | bytes 2097152 | tf_op jit(solution)/shard_map/psum | solution.py:169
  211.2 4.3 copy-start.36
  215.5 3.6 copy-start.43
  224.9 20.6 %collective-permute-start = (bf16[128,4096]{1,0:T(8,128)(2,1)}, bf16[128,4096]{1,0:T(8,128)(2,1)}, u32[]{:S(2)}, u32[]{:S(2)}) collective-permute-start(bf16[128,4096]{1,0:T(8,128)(2,1)} %get-tuple-element.111), channel_id=1, source_target_pairs={{0,64},{64,0},{1,65},{65,1},{2,66},{66,2},{3,67},{67,3},{4,68},{68... | collective-permute-start | bytes 3145736 | tf_op jit(solution)/shard_map/ppermute | solution.py:12
  252.5 5.3 copy-start.28
  273.4 3.9 copy-start.32
  282.3 3.4 copy-start.12
  282.3 3.4 copy-start.29
  282.3 4.5 copy-start.33
  282.3 4.5 copy-start.48
  303.9 244.5 %all-reduce.8.cloned.1.call-start = ((), (), s32[]{:S(2)}) async-start(), calls=%async_computation.4 | async-start | bytes 2097152 | tf_op jit(solution)/shard_map/psum | solution.py:169
  304.0 6.2 copy-start.1
  304.7 7.4 copy-start.22
  306.3 7.3 copy-start.21
  387.3 20.3 %collective-permute-start.1 = (bf16[128,4096]{1,0:T(8,128)(2,1)S(1)}, bf16[128,4096]{1,0:T(8,128)(2,1)S(1)}, u32[]{:S(2)}, u32[]{:S(2)}) collective-permute-start(bf16[128,4096]{1,0:T(8,128)(2,1)S(1)} %fusion.67), channel_id=1, source_target_pairs={{0,64},{64,0},{1,65},{65,1},{2,66},{66,2},{3,67},{67,3},{4,68},{68... | collective-permute-start | bytes 3145736 | tf_op jit(solution)/shard_map/ppermute | solution.py:12
  392.4 15.2 %copy-start.4 = (bf16[2,128,4096]{2,1,0:T(8,128)(2,1)S(1)}, bf16[2,128,4096]{2,1,0:T(8,128)(2,1)}, u32[]{:S(2)}) copy-start(bf16[2,128,4096]{2,1,0:T(8,128)(2,1)} %param.15) | copy-start | bytes 6291460
  392.4 15.2 %copy-start.42 = (f32[128]{0:T(128)S(1)}, f32[128]{0:T(128)}, u32[]{:S(2)}) copy-start(f32[128]{0:T(128)} %add_rsqrt_fusion.1) | copy-start | bytes 1540
  392.4 15.2 %copy-start.46 = (bf16[128]{0:T(256)(128)(2,1)S(1)}, bf16[128]{0:T(256)(128)(2,1)}, u32[]{:S(2)}) copy-start(bf16[128]{0:T(256)(128)(2,1)} %compare_convert_fusion.1) | copy-start | bytes 772
  413.4 5.3 copy-start.26
  423.4 5.6 copy-start.27
  445.3 2.5 copy-start.31
  465.7 6.0 copy-start.18
  465.7 364.2 %reduce-scatter.2.cloned.1.call-start = ((), (), s32[]{:S(2)}) async-start(), calls=%async_computation.5 | async-start | bytes 18874368 | tf_op jit(solution)/shard_map/reduce_scatter | solution.py:201
  466.3 7.0 copy-start.24
  466.3 8.5 %copy-start.23 = (bf16[1,128,512]{2,1,0:T(8,128)(2,1)S(1)}, bf16[1,128,512]{2,1,0:T(8,128)(2,1)}, u32[]{:S(2)}) copy-start(bf16[1,128,512]{2,1,0:T(8,128)(2,1)} %copy.138) | copy-start | bytes 393220
  550.0 20.7 %collective-permute-start.2 = (bf16[128,4096]{1,0:T(8,128)(2,1)S(1)}, bf16[128,4096]{1,0:T(8,128)(2,1)S(1)}, u32[]{:S(2)}, u32[]{:S(2)}) collective-permute-start(bf16[128,4096]{1,0:T(8,128)(2,1)S(1)} %fusion.77), channel_id=1, source_target_pairs={{0,64},{64,0},{1,65},{65,1},{2,66},{66,2},{3,67},{67,3},{4,68},{68... | collective-permute-start | bytes 3145736 | tf_op jit(solution)/shard_map/ppermute | solution.py:12
  555.5 15.2 %copy-start.5 = (bf16[2,128,4096]{2,1,0:T(8,128)(2,1)S(1)}, bf16[2,128,4096]{2,1,0:T(8,128)(2,1)}, u32[]{:S(2)}) copy-start(bf16[2,128,4096]{2,1,0:T(8,128)(2,1)} %param.15) | copy-start | bytes 6291460
  555.5 15.2 %copy-start.41 = (f32[128]{0:T(128)S(1)}, f32[128]{0:T(128)}, u32[]{:S(2)}) copy-start(f32[128]{0:T(128)} %add_rsqrt_fusion) | copy-start | bytes 1540
  555.5 15.2 %copy-start.45 = (bf16[128]{0:T(256)(128)(2,1)S(1)}, bf16[128]{0:T(256)(128)(2,1)}, u32[]{:S(2)}) copy-start(bf16[128]{0:T(256)(128)(2,1)} %compare_convert_fusion) | copy-start | bytes 772
  576.5 3.2 copy-start.25
  576.5 3.2 copy-start.47
  579.5 6.4 copy-start.30
  579.5 2.4 copy-start.7
  579.5 2.4 copy-start.35
  581.9 4.0 copy-start.2
  585.9 7.0 copy-start.9
  589.5 9.8 %copy-start.11 = (f32[1,8,128,128]{2,3,1,0:T(8,128)S(1)}, f32[1,8,128,128]{2,3,1,0:T(8,128)}, u32[]{:S(2)}) copy-start(f32[1,8,128,128]{2,3,1,0:T(8,128)} %constant_dynamic-slice_fusion.13) | copy-start | bytes 1572868
  595.5 5.5 copy-start.19
  595.5 5.5 copy-start.17
  621.5 5.7 copy-start.34
  635.1 9.2 %copy-start.20 = (bf16[8,64,128]{2,1,0:T(8,128)(2,1)S(1)}, bf16[8,64,128]{2,1,0:T(8,128)(2,1)}, u32[]{:S(2)}) copy-start(bf16[8,64,128]{2,1,0:T(8,128)(2,1)} %copy-done.19) | copy-start | bytes 393220
  699.7 29.4 %copy-start.40 = (f32[2]{0:T(128)}, f32[2]{0:T(128)S(1)}, u32[]{:S(2)}) copy-start(f32[2]{0:T(128)S(1)} %add_divide_fusion) | copy-start | bytes 28
  (9 other events, 12.6 us)
Sparse Core Ops, SparseCore 0:
  10.7 88.7 all-gather.1
  135.7 75.4 all-reduce.3
  304.0 81.6 all-reduce.5
  465.8 82.5 all-reduce.7
  729.2 100.5 reduce-scatter.1
where the time goes:
time: 857 us; the launch traced here: 846 us
  waiting for transfers between devices  395 us (46%)
  matrix products  202 us (24%)
  other arithmetic  95.5 us (11%)
  local copies, waits for them, and re-layouts  91.1 us (11%)
  blocking collectives  31.8 us (4%)
  between operations  22.1 us (3%)
    psum x3, waiting for transfers between devices, per_device(): lax.psum(relay_term.astype(jnp.bfloat16), 'mp').astype(jnp.float32)  206 us
    reduce_scatter x1, waiting for transfers between devices, per_device(): lax.psum_scatter(totals.astype(jnp.bfloat16), 'dp', scatter_dimension=0,...  101 us
    all_gather x1, waiting for transfers between devices, per_device(): gathered = lax.all_gather(weights, 'dp', axis=1, tiled=True)[0]  60.7 us
    dot_general x16, matrix products, project(): jnp.dot(left, right, preferred_element_type=jnp.float32)  55 us
    dynamic_update_slice x25, other arithmetic, put_row(): lax.dynamic_update_index_in_dim(buffer, jnp.where(valid, value, current),...  45.1 us
    dot_general x28, matrix products, gram(): return jnp.dot(matrix, matrix.T, preferred_element_type=jnp.float32)  42.7 us
    dynamic_slice x35, local copies, waits for them, and re-layouts, get_row(): return lax.dynamic_index_in_dim(buffer, index, 0, keepdims=False)  37.2 us
    psum x1, blocking collectives, per_device(): sq_norm = lax.psum(norm_parts, ('section', 'mp'))  31.8 us
  transfers between devices with their start and end apart: 8, of which 8 were waited for; matrix products, arithmetic and copies ran while one was open for 10% of the time, Pallas kernels for 0%

commit v1 on v0

--- a/solution.py
+++ b/solution.py
@@ -6,6 +6,10 @@
 D = 4096
 HEADS = 64
 HEAD = 64
+
+
+def run_wall(in_array):
+    return jnp.sum(lax.all_gather(in_array, "mp"), 0)
 
 
 def from_partner(x, axis, distance):
@@ -166,7 +170,7 @@
                 ),
             )
             residual = jnp.where(is_dec, 0.0, rows_now.astype(jnp.float32))
-            summed_rows = lax.psum(relay_term.astype(jnp.bfloat16), "mp").astype(jnp.float32)
+            summed_rows = run_wall(relay_term.astype(jnp.bfloat16)).astype(jnp.float32)
             payload = (summed_rows + residual).astype(jnp.bfloat16)
             incoming = from_partner(payload, "section", 0)
     sq_norm = lax.psum(norm_parts, ("section", "mp"))

time: 857 us -> 899 us (1.049)
  waiting for transfers between devices: 395 us -> 414 us
  other arithmetic: 95.5 us -> 113 us
  local copies, waits for them, and re-layouts: 91.1 us -> 101 us
    psum x3 -> x0, waiting for transfers between devices: 206 us -> none  [per_device(): lax.psum(relay_term.astype(jnp.bfloat16), 'mp').astype(jnp.float32)]
    all_gather x0 -> x3, waiting for transfers between devices: none -> 186 us  [run_wall(): return jnp.sum(lax.all_gather(in_array, 'mp'), 0)]
    all_gather x1, waiting for transfers between devices: 60.7 us -> 85.2 us  [per_device(): gathered = lax.all_gather(weights, 'dp', axis=1, tiled=True)[0]]
    ppermute x3, waiting for transfers between devices: 27.6 us -> 46.2 us  [from_partner(): lax.ppermute(x, axis, [(i, i ^ 1 << distance) for i in range(lax.axis_siz...]
    reduce_sum x0 -> x3, other arithmetic: none -> 18.4 us  [run_wall(): return jnp.sum(lax.all_gather(in_array, 'mp'), 0)]
  transfers between devices with their start and end apart: 8 -> 8, of which waited for: 8 -> 8; matrix products, arithmetic and copies ran while one was open for 10% -> 14% of each run, Pallas kernels for 0% -> 0%
where the time goes in v1:
time: 899 us; the launch traced here: 889 us
  waiting for transfers between devices  414 us (46%)
  matrix products  200 us (22%)
  other arithmetic  113 us (13%)
  local copies, waits for them, and re-layouts  101 us (11%)
  blocking collectives  30.3 us (3%)
  between operations  22.4 us (2%)
    all_gather x3, waiting for transfers between devices, run_wall(): return jnp.sum(lax.all_gather(in_array, 'mp'), 0)  186 us
    reduce_scatter x1, waiting for transfers between devices, per_device(): lax.psum_scatter(totals.astype(jnp.bfloat16), 'dp', scatter_dimension=0,...  96.1 us
    all_gather x1, waiting for transfers between devices, per_device(): gathered = lax.all_gather(weights, 'dp', axis=1, tiled=True)[0]  85.2 us
    dot_general x16, matrix products, project(): jnp.dot(left, right, preferred_element_type=jnp.float32)  55.6 us
    ppermute x3, waiting for transfers between devices, from_partner(): lax.ppermute(x, axis, [(i, i ^ 1 << distance) for i in range(lax.axis_siz...  46.2 us
    dynamic_update_slice x25, other arithmetic, put_row(): lax.dynamic_update_index_in_dim(buffer, jnp.where(valid, value, current),...  44.8 us
    dynamic_slice x35, local copies, waits for them, and re-layouts, get_row(): return lax.dynamic_index_in_dim(buffer, index, 0, keepdims=False)  42.2 us
    dot_general x28, matrix products, gram(): return jnp.dot(matrix, matrix.T, preferred_element_type=jnp.float32)  36.5 us
  transfers between devices with their start and end apart: 8, of which 8 were waited for; matrix products, arithmetic and copies ran while one was open for 14% of the time, Pallas kernels for 0%

profile of v1, /device:TPU:1, one launch (start us, length us, event | category | flops | bytes accessed | tf_op | source)
XLA Modules:
  0.0 889.2 jit_solution(10787314854302616078)
XLA Ops:
  7.2 3.3 copy.83
  14.2 85.2 %all-gather.8.cloned.1.call-done = bf16[1,4096,4,512]{3,1,2,0:T(8,128)(2,1)} async-done(((bf16[1,512,4,512]{3,1,2,0:T(8,128)(2,1)}), bf16[1,4096,4,512]{3,1,2,0:T(8,128)(2,1)}) %all-gather.8.cloned.1.call-update) | async-done | bytes 16777232 | tf_op jit(solution)/shard_map/all_gather | solution.py:98
  100.2 3.6 bitcast_dynamic-update-slice_fusion.20
  103.9 3.0 bitcast_dynamic-update-slice_fusion.21
  109.0 3.3 fusion.125
  112.5 3.0 bitcast_dynamic-update-slice_fusion.19
  126.4 4.8 conditional.3
  126.4 4.8 fusion
  160.0 66.7 %all-gather.10.cloned.1.call-done = bf16[1024,4096]{1,0:T(8,128)(2,1)} async-done(((bf16[128,4096]{1,0:T(8,128)(2,1)}), bf16[1024,4096]{1,0:T(8,128)(2,1)}) %all-gather.10.cloned.1.call-update) | async-done | bytes 8388624 | tf_op jit(solution)/shard_map/all_gather | solution.py:12
  226.8 6.1 reduce_sum.258
  232.9 3.7 fusion.60
  239.3 3.6 bitcast_dynamic-update-slice_fusion.17
  251.4 11.2 %collective-permute-done = bf16[128,4096]{1,0:T(8,128)(2,1)} collective-permute-done((bf16[128,4096]{1,0:T(8,128)(2,1)}, bf16[128,4096]{1,0:T(8,128)(2,1)}, u32[]{:S(2)}, u32[]{:S(2)}) %collective-permute-start) | collective-permute-done | bytes 1048608 | tf_op jit(solution)/shard_map/ppermute | solution.py:16
  262.6 6.0 bitcast_dynamic-update-slice_fusion.5
  269.6 3.6 fusion.138
  279.6 3.8 bitcast_dynamic-update-slice_fusion.16
  284.2 3.9 fusion.126
  308.7 4.8 conditional.4
  308.7 4.8 fusion.8
  333.2 75.7 %all-gather.12.cloned.1.call-done = bf16[1024,4096]{1,0:T(8,128)(2,1)} async-done(((bf16[128,4096]{1,0:T(8,128)(2,1)}), bf16[1024,4096]{1,0:T(8,128)(2,1)}) %all-gather.12.cloned.1.call-update) | async-done | bytes 8388624 | tf_op jit(solution)/shard_map/all_gather | solution.py:12
  408.9 6.1 reduce_sum.261
  424.4 17.5 %collective-permute-done.1 = bf16[128,4096]{1,0:T(8,128)(2,1)S(1)} collective-permute-done((bf16[128,4096]{1,0:T(8,128)(2,1)S(1)}, bf16[128,4096]{1,0:T(8,128)(2,1)S(1)}, u32[]{:S(2)}, u32[]{:S(2)}) %collective-permute-start.1) | collective-permute-done | bytes 1048608 | tf_op jit(solution)/shard_map/ppermute | solution.py:16
  442.0 4.8 bitcast_dynamic-update-slice_fusion.4
  447.8 3.6 fusion.139
  457.9 3.9 bitcast_dynamic-update-slice_fusion.13
  468.9 3.9 fusion.127
  486.5 4.9 conditional.5
  486.5 4.8 fusion.16
  542.9 44.0 %all-gather.14.cloned.1.call-done = bf16[1024,4096]{1,0:T(8,128)(2,1)} async-done(((bf16[128,4096]{1,0:T(8,128)(2,1)}), bf16[1024,4096]{1,0:T(8,128)(2,1)}) %all-gather.14.cloned.1.call-update) | async-done | bytes 8388624 | tf_op jit(solution)/shard_map/all_gather | solution.py:12
  586.9 6.1 reduce_sum.264
  602.7 17.5 %collective-permute-done.2 = bf16[128,4096]{1,0:T(8,128)(2,1)S(1)} collective-permute-done((bf16[128,4096]{1,0:T(8,128)(2,1)S(1)}, bf16[128,4096]{1,0:T(8,128)(2,1)S(1)}, u32[]{:S(2)}, u32[]{:S(2)}) %collective-permute-start.2) | collective-permute-done | bytes 1048608 | tf_op jit(solution)/shard_map/ppermute | solution.py:16
  620.2 4.8 bitcast_dynamic-update-slice_fusion.3
  626.0 3.0 fusion.140
  631.4 4.0 bitcast_dynamic-update-slice_fusion.11
  635.4 3.6 fusion.128
  653.9 5.7 convolution_bitcast_fusion.1
  659.6 5.7 convolution_bitcast_fusion.5
  665.3 5.7 convolution_bitcast_fusion.2
  671.0 5.7 convolution_bitcast_fusion.6
  678.7 5.9 convolution_bitcast_fusion
  684.7 5.7 convolution_bitcast_fusion.4
  703.3 5.7 convolution_bitcast_fusion.3
  711.5 5.8 convolution_bitcast_fusion.7
  717.3 30.3 %psum.7 = f32[2]{0:T(128)S(1)} all-reduce(f32[2]{0:T(128)S(1)} %and_select_fusion.3), channel_id=1, replica_groups=mesh['section'=2,'dp'=8,'mp'=8] {'section','mp'}, use_global_device_ids=true, to_apply=%region_37.38 | all-reduce | flops 2 | bytes 16 | tf_op jit(solution)/shard_map/psum | solution.py:176
  748.2 28.8 %fusion.33 = bf16[4096,4,512]{2,0,1:T(8,128)(2,1)} fusion(f32[4096,1,512]{2,0,1:T(8,128)} %convolution_bitcast_fusion.4, f32[4096,1,512]{2,0,1:T(8,128)} %convolution_bitcast_fusion.5, f32[4096,1,512]{2,0,1:T(8,128)} %convolution_bitcast_fusion.6, f32[4096,1,512]{2,0,1:T(8,128)} %convolution_bitcast_fusion.7, f32[4096,1,512]{2,0,1:T(8,128)} %convolution_bitcast_fusion, ...), kind=kLoop, calls=%fused_computation.37 | loop fusion | flops 83886080 | bytes 83886088 | tf_op jit(solution)/shard_map/convert_element_type | solution.py:206
  777.0 96.1 %reduce-scatter.2.cloned.1.call-done = bf16[512,4,512]{2,0,1:T(8,128)(2,1)} async-done(((bf16[4096,4,512]{2,0,1:T(8,128)(2,1)}), bf16[512,4,512]{2,0,1:T(8,128)(2,1)}) %reduce-scatter.2.cloned.1.call-update) | async-done | bytes 2097168 | tf_op jit(solution)/shard_map/reduce_scatter | solution.py:205
  873.1 4.4 fusion.35
  877.5 4.7 copy.145
  (305 shorter events, 233.4 us)
Async XLA Ops:
  7.2 92.3 %all-gather.8.cloned.1.call-start = ((), (), s32[]{:S(2)}) async-start(), calls=%async_computation.1 | async-start | bytes 18874368 | tf_op jit(solution)/shard_map/all_gather | solution.py:98
  10.6 216.2 %all-gather.10.cloned.1.call-start = ((), (), s32[]{:S(2)}) async-start(), calls=%async_computation.3 | async-start | bytes 9437184 | tf_op jit(solution)/shard_map/all_gather | solution.py:12
  14.2 94.9 %copy-start.50 = (bf16[128]{0:T(256)(128)(2,1)}, bf16[128]{0:T(256)(128)(2,1)S(1)}, u32[]{:S(2)}) copy-start(bf16[128]{0:T(256)(128)(2,1)S(1)} %compare_convert_fusion.3) | copy-start | bytes 772
  14.2 98.3 %copy-start.41 = (f32[128]{0:T(128)}, f32[128]{0:T(128)S(1)}, u32[]{:S(2)}) copy-start(f32[128]{0:T(128)S(1)} %add_rsqrt_fusion.3) | copy-start | bytes 1540
  106.9 46.0 %copy-start.8 = (bf16[2,128,512]{2,1,0:T(8,128)(2,1)}, bf16[2,128,512]{2,1,0:T(8,128)(2,1)S(1)}, u32[]{:S(2)}) copy-start(bf16[2,128,512]{2,1,0:T(8,128)(2,1)S(1)} %get-tuple-element.148) | copy-start | bytes 786436
  112.4 8.8 copy-start.15
  115.4 5.8 copy-start.6
  131.2 277.6 %all-gather.12.cloned.1.call-start = ((), (), s32[]{:S(2)}) async-start(), calls=%async_computation.4 | async-start | bytes 9437184 | tf_op jit(solution)/shard_map/all_gather | solution.py:12
  131.5 4.0 copy-start.42
  135.5 4.0 copy-start.3
  135.5 4.0 copy-start.51
  152.9 4.3 copy-start.13
  232.9 6.3 copy-start.39
  236.7 6.2 copy-start.48
  236.7 25.9 %collective-permute-start = (bf16[128,4096]{1,0:T(8,128)(2,1)}, bf16[128,4096]{1,0:T(8,128)(2,1)}, u32[]{:S(2)}, u32[]{:S(2)}) collective-permute-start(bf16[128,4096]{1,0:T(8,128)(2,1)} %get-tuple-element.111), channel_id=1, source_target_pairs={{0,64},{64,0},{1,65},{65,1},{2,66},{66,2},{3,67},{67,3},{4,68},{68... | collective-permute-start | bytes 3145736 | tf_op jit(solution)/shard_map/ppermute | solution.py:16
  248.1 20.5 %copy-start.33 = (bf16[128,512]{1,0:T(8,128)(2,1)}, bf16[128,512]{1,0:T(8,128)(2,1)S(1)}, u32[]{:S(2)}) copy-start(bf16[128,512]{1,0:T(8,128)(2,1)S(1)} %fusion.131) | copy-start | bytes 393220
  269.6 5.3 copy-start.35
  289.1 13.0 %copy-start.17 = (bf16[128,512]{0,1:T(8,128)(2,1)}, bf16[128,512]{0,1:T(8,128)(2,1)S(1)}, u32[]{:S(2)}) copy-start(bf16[128,512]{0,1:T(8,128)(2,1)S(1)} %copy.98) | copy-start | bytes 393220
  313.5 273.4 %all-gather.14.cloned.1.call-start = ((), (), s32[]{:S(2)}) async-start(), calls=%async_computation.5 | async-start | bytes 9437184 | tf_op jit(solution)/shard_map/all_gather | solution.py:12
  416.5 25.5 %collective-permute-start.1 = (bf16[128,4096]{1,0:T(8,128)(2,1)S(1)}, bf16[128,4096]{1,0:T(8,128)(2,1)S(1)}, u32[]{:S(2)}, u32[]{:S(2)}) collective-permute-start(bf16[128,4096]{1,0:T(8,128)(2,1)S(1)} %fusion.67), channel_id=1, source_target_pairs={{0,64},{64,0},{1,65},{65,1},{2,66},{66,2},{3,67},{67,3},{4,68},{68... | collective-permute-start | bytes 3145736 | tf_op jit(solution)/shard_map/ppermute | solution.py:16
  421.6 20.3 %copy-start.4 = (bf16[2,128,4096]{2,1,0:T(8,128)(2,1)S(1)}, bf16[2,128,4096]{2,1,0:T(8,128)(2,1)}, u32[]{:S(2)}) copy-start(bf16[2,128,4096]{2,1,0:T(8,128)(2,1)} %param.15) | copy-start | bytes 6291460
  421.6 20.3 %copy-start.47 = (f32[128]{0:T(128)S(1)}, f32[128]{0:T(128)}, u32[]{:S(2)}) copy-start(f32[128]{0:T(128)} %copy-done.46) | copy-start | bytes 1540
  421.6 20.3 %copy-start.53 = (bf16[128]{0:T(256)(128)(2,1)S(1)}, bf16[128]{0:T(256)(128)(2,1)}, u32[]{:S(2)}) copy-start(bf16[128]{0:T(256)(128)(2,1)} %compare_convert_fusion.1) | copy-start | bytes 772
  477.8 3.4 copy-start.18
  491.5 381.6 %reduce-scatter.2.cloned.1.call-start = ((), (), s32[]{:S(2)}) async-start(), calls=%async_computation.2 | async-start | bytes 18874368 | tf_op jit(solution)/shard_map/reduce_scatter | solution.py:205
  514.3 5.1 copy-start.31
  514.3 6.7 copy-start.30
  514.3 8.3 copy-start.24
  514.3 8.3 copy-start.55
  514.5 13.7 %copy-start.10 = (bf16[128,8,64]{0,2,1:T(8,128)(2,1)S(1)}, bf16[128,8,64]{0,2,1:T(8,128)(2,1)}, u32[]{:S(2)}) copy-start(bf16[128,8,64]{0,2,1:T(8,128)(2,1)} %convolution_bitcast_fusion.8) | copy-start | bytes 393220
  531.1 5.9 copy-start.1
  533.9 4.2 copy-start.28
  534.2 5.5 copy-start.29
  534.4 6.9 copy-start.27
  594.5 25.7 %collective-permute-start.2 = (bf16[128,4096]{1,0:T(8,128)(2,1)S(1)}, bf16[128,4096]{1,0:T(8,128)(2,1)S(1)}, u32[]{:S(2)}, u32[]{:S(2)}) collective-permute-start(bf16[128,4096]{1,0:T(8,128)(2,1)S(1)} %fusion.77), channel_id=1, source_target_pairs={{0,64},{64,0},{1,65},{65,1},{2,66},{66,2},{3,67},{67,3},{4,68},{68... | collective-permute-start | bytes 3145736 | tf_op jit(solution)/shard_map/ppermute | solution.py:16
  599.9 20.3 %copy-start.5 = (bf16[2,128,4096]{2,1,0:T(8,128)(2,1)S(1)}, bf16[2,128,4096]{2,1,0:T(8,128)(2,1)}, u32[]{:S(2)}) copy-start(bf16[2,128,4096]{2,1,0:T(8,128)(2,1)} %param.15) | copy-start | bytes 6291460
  599.9 20.3 %copy-start.45 = (f32[128]{0:T(128)S(1)}, f32[128]{0:T(128)}, u32[]{:S(2)}) copy-start(f32[128]{0:T(128)} %copy-done.44) | copy-start | bytes 1540
  599.9 20.3 %copy-start.52 = (bf16[128]{0:T(256)(128)(2,1)S(1)}, bf16[128]{0:T(256)(128)(2,1)}, u32[]{:S(2)}) copy-start(bf16[128]{0:T(256)(128)(2,1)} %compare_convert_fusion) | copy-start | bytes 772
  626.0 3.2 copy-start.54
  629.0 6.4 copy-start.36
  631.4 4.0 copy-start.2
  635.4 7.0 copy-start.9
  639.0 9.7 %copy-start.14 = (f32[1,8,128,128]{2,3,1,0:T(8,128)S(1)}, f32[1,8,128,128]{2,3,1,0:T(8,128)}, u32[]{:S(2)}) copy-start(f32[1,8,128,128]{2,3,1,0:T(8,128)} %constant_dynamic-slice_fusion.13) | copy-start | bytes 1572868
  645.0 5.5 copy-start.25
  645.0 5.5 copy-start.23
  671.0 5.7 copy-start.37
  684.7 9.1 %copy-start.26 = (bf16[8,64,128]{2,1,0:T(8,128)(2,1)S(1)}, bf16[8,64,128]{2,1,0:T(8,128)(2,1)}, u32[]{:S(2)}) copy-start(bf16[8,64,128]{2,1,0:T(8,128)(2,1)} %copy-done.25) | copy-start | bytes 393220
  747.5 29.4 %copy-start.43 = (f32[2]{0:T(128)}, f32[2]{0:T(128)S(1)}, u32[]{:S(2)}) copy-start(f32[2]{0:T(128)S(1)} %add_divide_fusion) | copy-start | bytes 28
  (15 other events, 26.2 us)
Sparse Core Ops, SparseCore 0:
  10.7 88.7 all-gather.7
  131.3 95.3 all-gather.9
  313.6 95.1 all-gather.11
  491.6 95.2 all-gather.13
  777.1 95.9 reduce-scatter.1
